TPU v7x, 512 devices: a whole 4x4x16 slice. The times are simulated.
512 devices in a mesh: query: 32 (over z, core), passage: 16 (over x, y).
Axes of the slice: x: 4, y: 4, z: 16, core: 2. Of those that a mesh axis runs over, the one named last changes fastest.
Arguments:
- queries: bfloat16 [2048, 32, 128], P(('query', 'passage')), may hold values from -60 to 60
- hidden: bfloat16 [2048, 180, 768], P(('query', 'passage')), may hold values from -24 to 24
- proj: bfloat16 [768, 128], replicated, may hold values from -0.21875 to 0.21875
- lists: int32 [2048, 64], P(('query', 'passage')), may hold values from 0 to 63
Outputs:
- losses: float32 [2048], P(('query', 'passage'))
- w_grad: float32 [768, 128], P('passage')
Inputs may be any that keep to these rules, and one draw needn't show every extreme that they name: `lists`: queries of one row only list passages of that same row; entry 0 of each list is the query's positive passage.
All inputs are finite; a program needn't handle non-finite values.
Results may differ from a plain program's by a relative error of at most 0.0075.
The roundings to bfloat16 on the way count: a program that leaves them out, or rounds other values in their place, can miss the bound.
Values may be sent and summed in bfloat16 or wider, within the bound.
A program may use at most 64 MiB of HBM per device.

v0:
```python
import jax
import jax.numpy as jnp
from jax import lax
from jax.sharding import PartitionSpec as P

BETA = 4.0
EPS = 1e-06


def body(queries, hidden, proj, lists):
    qcount, qtok, width = queries.shape
    pcount, ptok, hwidth = hidden.shape
    nside = lax.axis_size("passage")
    prow = pcount * nside
    total = qcount * lax.axis_size("query") * nside
    hidden_flat = hidden.reshape(-1, hwidth)
    flat = jnp.dot(hidden_flat, proj, preferred_element_type=jnp.float32)
    norm = jnp.sqrt(jnp.sum(flat * flat, axis=1, keepdims=True) + EPS)
    unit = flat / norm
    embed = unit.astype(jnp.bfloat16).reshape(pcount, ptok, width)
    gathered = lax.all_gather(queries, "passage", axis=0, tiled=True)
    qflat = gathered.reshape(-1, width)

    def score_single(emb):
        sims = lax.dot_general(
            emb, qflat, (((1,), (1,)), ((), ())), preferred_element_type=jnp.float32
        )
        lse = jax.nn.logsumexp(BETA * sims, axis=0)
        return jnp.sum(lse.reshape(-1, qtok), axis=1) / BETA

    scores = lax.map(score_single, embed).T
    mine = lax.all_to_all(scores, "passage", split_axis=0, concat_axis=1, tiled=True)
    columns = jnp.arange(prow, dtype=jnp.int32)
    onehot = (lists[:, :, None] == columns[None, None, :]).astype(jnp.float32)
    listed = jnp.einsum("qkp,qp->qk", onehot, mine, precision=lax.Precision.HIGHEST)
    losses = jax.nn.logsumexp(listed, axis=1) - listed[:, 0]
    probs = jax.nn.softmax(listed, axis=1)
    target = (jnp.arange(listed.shape[1], dtype=jnp.int32) == 0).astype(jnp.float32)
    coef = (
        jnp.einsum("qkp,qk->qp", onehot, probs - target[None, :], precision=lax.Precision.HIGHEST)
        / total
    )
    coef_home = lax.all_to_all(coef, "passage", split_axis=1, concat_axis=0, tiled=True)
    grad_qflat = gathered.reshape(-1, width)

    def grad_single(args):
        emb, column = args
        sims = lax.dot_general(
            emb, grad_qflat, (((1,), (1,)), ((), ())), preferred_element_type=jnp.float32
        )
        probs = jax.nn.softmax(BETA * sims, axis=0)
        weight = (probs * jnp.repeat(column, qtok)[None, :]).astype(jnp.bfloat16)
        return jnp.dot(weight, grad_qflat, preferred_element_type=jnp.float32)

    d_embed = lax.map(grad_single, (embed, coef_home.T))
    d_rows = d_embed.reshape(-1, width)
    d_flat = ((d_rows - unit * jnp.sum(d_rows * unit, axis=1, keepdims=True)) / norm).astype(
        jnp.bfloat16
    )
    partial_grad = lax.dot_general(
        hidden_flat, d_flat, (((0,), (0,)), ((), ())), preferred_element_type=jnp.float32
    )
    share = hwidth // nside
    full_grad = lax.psum(partial_grad, ("query", "passage"))
    w_grad = lax.dynamic_slice_in_dim(full_grad, lax.axis_index("passage") * share, share, 0)
    return (losses, w_grad)


def solution(mesh):
    placed = (
        P(("query", "passage"), None, None),
        P(("query", "passage"), None, None),
        P(),
        P(("query", "passage"), None),
    )
    return jax.shard_map(
        body,
        mesh=mesh,
        in_specs=placed,
        out_specs=(P(("query", "passage")), P("passage", None)),
        check_vma=False,
    )
```

profile of v0, /device:TPU:2, one launch (start us, length us, event | category | flops | bytes accessed | tf_op | source)
XLA Modules:
  0.0 561.4 jit_solution(6270691283780664740)
XLA Ops:
  7.2 1.4 copy.11
  10.2 26.8 %all_gather.3 = bf16[64,32,128]{2,1,0:T(8,128)(2,1)S(1)} all-gather(bf16[4,32,128]{2,1,0:T(8,128)(2,1)S(1)} %copy-done.6), channel_id=1, replica_groups=mesh['query'=32,'passage'=16] {'passage'}, dimensions={0}, use_global_device_ids=true | all-gather | bytes 557056 | tf_op jit(solution)/shard_map/all_gather | solution.py:21
  37.0 4.4 while.20
  42.1 5.4 all-to-all-start
  47.6 6.2 %all-to-all-done = f32[16,4,4]{1,2,0:T(4,128)S(1)} async-done(((f32[16,4,4]{1,2,0:T(4,128)}), f32[16,4,4]{1,2,0:T(4,128)S(1)}, u32[]{:S(2)}, u32[]{:S(2)}) %all-to-all-start) | async-done | bytes 1056 | tf_op jit(solution)/shard_map/all_to_all | solution.py:32
  55.5 0.6 copy.14
  56.1 4.8 all-to-all-start.1
  60.9 6.2 %all-to-all-done.1 = f32[4,16,4]{2,0,1:T(4,128)S(1)} async-done(((f32[4,16,4]{2,0,1:T(4,128)}), f32[4,16,4]{2,0,1:T(4,128)S(1)}, u32[]{:S(2)}, u32[]{:S(2)}) %all-to-all-start.1) | async-done | bytes 1056 | tf_op jit(solution)/shard_map/all_to_all | solution.py:43
  67.2 16.0 %while.21 = (s32[]{:T(128)}, f32[4,180,128]{2,1,0:T(8,128)}, bf16[4,180,128]{2,1,0:T(8,128)(2,1)S(1)}, bf16[2048,128]{1,0:T(8,128)(2,1)S(1)}, f32[4,64]{1,0:T(4,128)S(1)}, /*index=5*/s32[]{:T(128)}) while((s32[]{:T(128)}, f32[4,180,128]{2,1,0:T(8,128)}, bf16[4,180,128]{2,1,0:T(8,128)(2,1)S(1)}, bf16[2048,128]{1,0:T(8,128)(2,1)S(1)}, ...), condition=%wide.region_12.13_spmd, body=%wide.region_9.0_spmd.sunk | while | flops 191688704 | bytes 5761993 | solution.py:55
  67.2 1.1 fusion.44
  68.4 0.7 mul.57
  69.1 1.0 fusion.46
  70.1 1.1 fusion.47
  71.2 1.1 fusion.44
  72.4 0.7 mul.57
  73.1 1.0 fusion.46
  74.1 1.1 fusion.47
  75.2 1.1 fusion.44
  76.4 0.7 mul.57
  77.1 1.0 fusion.46
  78.1 1.1 fusion.47
  79.3 1.1 fusion.44
  80.5 0.7 mul.57
  81.1 1.0 fusion.46
  82.2 1.1 fusion.47
  83.3 1.0 reshape.67
  84.3 1.3 multiply_reduce_fusion
  85.6 2.3 convolution_bitcast_fusion.1
  88.0 1.2 fusion.18
  89.2 463.7 %all-reduce.2.cloned.1.call-done = f32[768,128]{0,1:T(8,128)} async-done(((f32[768,128]{0,1:T(8,128)}), f32[768,128]{0,1:T(8,128)}) %all-reduce.2.cloned.1.call-update) | async-done | bytes 393232 | tf_op jit(solution)/shard_map/psum | solution.py:64
  552.8 1.0 constant_dynamic-slice_fusion.1
  553.8 0.7 copy.16
  (118 shorter events, 8.6 us)
Async XLA Ops:
  7.2 1.7 copy-start
  8.9 1.3 copy-start.6
  9.4 0.7 copy-start.1
  9.5 0.7 copy-start.5
  37.0 16.8 %copy-start.12 = (s32[4,64]{1,0:T(4,128)S(1)}, s32[4,64]{1,0:T(4,128)}, u32[]{:S(2)}) copy-start(s32[4,64]{1,0:T(4,128)} %param.11) | copy-start | bytes 3076
  42.1 11.6 %all-to-all-start = ((f32[16,4,4]{1,2,0:T(4,128)}), f32[16,4,4]{1,2,0:T(4,128)S(1)}, u32[]{:S(2)}, u32[]{:S(2)}) async-start(f32[16,4,4]{1,2,0:T(4,128)} %copy.12), calls=%async_computation | async-start | bytes 65536 | tf_op jit(solution)/shard_map/all_to_all | solution.py:32
  54.2 13.0 %copy-start.3 = (f32[4,1,64]{0,2,1:T(8,128)}, f32[4,1,64]{0,2,1:T(8,128)S(1)}, u32[]{:S(2)}) copy-start(f32[4,1,64]{0,2,1:T(8,128)S(1)} %copy.18) | copy-start | bytes 3076
  54.3 0.6 copy-start.7
  56.1 11.1 %all-to-all-start.1 = ((f32[4,16,4]{2,0,1:T(4,128)}), f32[4,16,4]{2,0,1:T(4,128)S(1)}, u32[]{:S(2)}, u32[]{:S(2)}) async-start(f32[4,16,4]{2,0,1:T(4,128)} %copy.14), calls=%async_computation.1 | async-start | bytes 65536 | tf_op jit(solution)/shard_map/all_to_all | solution.py:43
  60.8 492.0 %all-reduce.2.cloned.1.call-start = ((), (), s32[]{:S(2)}) async-start(), calls=%async_computation.2 | async-start | bytes 786432 | tf_op jit(solution)/shard_map/psum | solution.py:64
  67.2 1.1 copy-start.10
  69.1 1.0 copy-start.2
  69.1 1.0 copy-start.4
  70.1 1.1 copy-start.11
  71.2 1.1 copy-start.10
  73.1 1.0 copy-start.2
  73.1 1.0 copy-start.4
  74.1 1.1 copy-start.11
  75.2 1.1 copy-start.10
  77.1 1.0 copy-start.2
  77.1 1.0 copy-start.4
  78.1 1.1 copy-start.11
  79.3 1.1 copy-start.10
  81.1 1.0 copy-start.2
  81.1 1.0 copy-start.4
  82.1 1.1 copy-start.11
  85.6 2.4 copy-start.8
  85.6 2.4 copy-start.9
Sparse Core Ops, SparseCore 0:
  88.1 464.7 all-reduce.1
where the time goes:
time: 562 us; the launch traced here: 561 us
  waiting for transfers between devices  476 us (85%)
  blocking collectives  26.8 us (5%)
  matrix products  14.4 us (3%)
  between operations  14.2 us (3%)
  local copies, waits for them, and re-layouts  10.5 us (2%)
  starting transfers between devices  10.2 us (2%)
  other arithmetic  8.8 us (2%)
    psum x1, waiting for transfers between devices, body(): full_grad = lax.psum(partial_grad, ('query', 'passage'))  464 us
    all_gather x1, blocking collectives, body(): gathered = lax.all_gather(queries, 'passage', axis=0, tiled=True)  26.8 us
  transfers between devices with their start and end apart: 3, of which 3 were waited for; matrix products, arithmetic and copies ran while one was open for 0% of the time, Pallas kernels for 0%

commit v1 on v0

--- a/solution.py
+++ b/solution.py
@@ -2,6 +2,7 @@
 import jax.numpy as jnp
 from jax import lax
 from jax.sharding import PartitionSpec as P
+from jax.lax import psum
 
 BETA = 4.0
 EPS = 1e-06
@@ -61,7 +62,11 @@
         hidden_flat, d_flat, (((0,), (0,)), ((), ())), preferred_element_type=jnp.float32
     )
     share = hwidth // nside
-    full_grad = lax.psum(partial_grad, ("query", "passage"))
+
+    def follow_lines(packet):
+        return psum(psum(packet, "query"), axis_name="passage")
+
+    full_grad = follow_lines(partial_grad)
     w_grad = lax.dynamic_slice_in_dim(full_grad, lax.axis_index("passage") * share, share, 0)
     return (losses, w_grad)
 

time: 562 us -> 414 us (0.74)
  the two profiles are of different devices: /device:TPU:2 before, /device:TPU:32 now
where the time goes in v1:
time: 414 us; the launch traced here: 413 us
  waiting for transfers between devices  333 us (80%)
  blocking collectives  24.3 us (6%)
  matrix products  14.3 us (3%)
  between operations  14.2 us (3%)
  local copies, waits for them, and re-layouts  10.5 us (3%)
  other arithmetic  8.73 us (2%)
  starting transfers between devices  8.49 us (2%)
    psum x2, waiting for transfers between devices, follow_lines(): return psum(psum(packet, 'query'), axis_name='passage')  317 us
    all_gather x1, blocking collectives, body(): gathered = lax.all_gather(queries, 'passage', axis=0, tiled=True)  24.3 us
  transfers between devices with their start and end apart: 4, of which 4 were waited for; matrix products, arithmetic and copies ran while one was open for 0% of the time, Pallas kernels for 0%

profile of v1, /device:TPU:32, one launch (start us, length us, event | category | flops | bytes accessed | tf_op | source)
XLA Modules:
  0.0 413.5 jit_solution(6533797748274947541)
XLA Ops:
  7.2 1.4 copy.11
  10.2 24.3 %all_gather.3 = bf16[64,32,128]{2,1,0:T(8,128)(2,1)S(1)} all-gather(bf16[4,32,128]{2,1,0:T(8,128)(2,1)S(1)} %copy-done.6), channel_id=1, replica_groups=mesh['query'=32,'passage'=16] {'passage'}, dimensions={0}, use_global_device_ids=true | all-gather | bytes 557056 | tf_op jit(solution)/shard_map/all_gather | solution.py:22
  34.5 4.4 %while.20 = (s32[]{:T(128)}, f32[4,64]{1,0:T(4,128)S(1)}, bf16[4,180,128]{2,1,0:T(8,128)(2,1)S(1)}, bf16[2048,128]{1,0:T(8,128)(2,1)S(1)}, s32[]{:T(128)}, /*index=5*/s32[]{:T(128)}) while((s32[]{:T(128)}, f32[4,64]{1,0:T(4,128)S(1)}, bf16[4,180,128]{2,1,0:T(8,128)(2,1)S(1)}, bf16[2048,128]{1,0:T(8,128)(2,1)S(1)}, s32[]{:T(128)}, ...), condition=%wide.region_5.6_spmd, body=%wide.region_1.5_spmd.sunk | while | flops 95856640 | bytes 3628373 | solution.py:32
  39.6 4.9 %all-to-all-start = ((f32[16,4,4]{1,2,0:T(4,128)}), f32[16,4,4]{1,2,0:T(4,128)S(1)}, u32[]{:S(2)}, u32[]{:S(2)}) async-start(f32[16,4,4]{1,2,0:T(4,128)} %copy.12), calls=%async_computation | async-start | bytes 65536 | tf_op jit(solution)/shard_map/all_to_all | solution.py:33
  44.5 7.6 %all-to-all-done = f32[16,4,4]{1,2,0:T(4,128)S(1)} async-done(((f32[16,4,4]{1,2,0:T(4,128)}), f32[16,4,4]{1,2,0:T(4,128)S(1)}, u32[]{:S(2)}, u32[]{:S(2)}) %all-to-all-start) | async-done | bytes 1056 | tf_op jit(solution)/shard_map/all_to_all | solution.py:33
  54.4 3.5 all-to-all-start.1
  57.9 7.5 %all-to-all-done.1 = f32[4,16,4]{2,0,1:T(4,128)S(1)} async-done(((f32[4,16,4]{2,0,1:T(4,128)}), f32[4,16,4]{2,0,1:T(4,128)S(1)}, u32[]{:S(2)}, u32[]{:S(2)}) %all-to-all-start.1) | async-done | bytes 1056 | tf_op jit(solution)/shard_map/all_to_all | solution.py:44
  65.5 16.0 %while.21 = (s32[]{:T(128)}, f32[4,180,128]{2,1,0:T(8,128)}, bf16[4,180,128]{2,1,0:T(8,128)(2,1)S(1)}, bf16[2048,128]{1,0:T(8,128)(2,1)S(1)}, f32[4,64]{1,0:T(4,128)S(1)}, /*index=5*/s32[]{:T(128)}) while((s32[]{:T(128)}, f32[4,180,128]{2,1,0:T(8,128)}, bf16[4,180,128]{2,1,0:T(8,128)(2,1)S(1)}, bf16[2048,128]{1,0:T(8,128)(2,1)S(1)}, ...), condition=%wide.region_12.13_spmd, body=%wide.region_9.0_spmd.sunk | while | flops 191688704 | bytes 5761993 | solution.py:56
  65.5 1.1 fusion.44
  66.7 0.7 mul.57
  67.4 1.0 fusion.46
  68.4 1.1 fusion.47
  69.5 1.1 fusion.44
  70.7 0.7 mul.57
  71.4 1.0 fusion.46
  72.4 1.1 fusion.47
  73.5 1.1 fusion.44
  74.7 0.7 mul.57
  75.4 1.0 fusion.46
  76.4 1.1 fusion.47
  77.5 1.1 fusion.44
  78.7 0.7 mul.57
  79.4 1.0 fusion.46
  80.4 1.1 fusion.47
  81.5 1.0 reshape.67
  82.5 1.3 multiply_reduce_fusion
  83.8 2.3 convolution_bitcast_fusion.1
  86.3 200.4 %all-reduce.3.cloned.1.call-done = f32[768,128]{0,1:T(8,128)} async-done(((f32[768,128]{0,1:T(8,128)}), f32[768,128]{0,1:T(8,128)}) %all-reduce.3.cloned.1.call-update) | async-done | bytes 393232 | tf_op jit(solution)/shard_map/psum | solution.py:67
  286.8 1.2 fusion.18
  288.0 117.0 %all-reduce.5.cloned.1.call-done = f32[768,128]{0,1:T(8,128)} async-done(((f32[768,128]{0,1:T(8,128)}), f32[768,128]{0,1:T(8,128)}) %all-reduce.5.cloned.1.call-update) | async-done | bytes 393232 | tf_op jit(solution)/shard_map/psum | solution.py:67
  405.0 1.0 constant_dynamic-slice_fusion.1
  405.9 0.7 copy.16
  (121 shorter events, 9.3 us)
Async XLA Ops:
  7.2 1.7 copy-start
  8.9 1.3 copy-start.6
  9.4 0.7 copy-start.1
  9.5 0.7 copy-start.5
  34.5 17.7 %copy-start.12 = (s32[4,64]{1,0:T(4,128)S(1)}, s32[4,64]{1,0:T(4,128)}, u32[]{:S(2)}) copy-start(s32[4,64]{1,0:T(4,128)} %param.11) | copy-start | bytes 3076
  39.6 12.6 %all-to-all-start = ((f32[16,4,4]{1,2,0:T(4,128)}), f32[16,4,4]{1,2,0:T(4,128)S(1)}, u32[]{:S(2)}, u32[]{:S(2)}) async-start(f32[16,4,4]{1,2,0:T(4,128)} %copy.12), calls=%async_computation | async-start | bytes 65536 | tf_op jit(solution)/shard_map/all_to_all | solution.py:33
  52.6 12.9 %copy-start.3 = (f32[4,1,64]{0,2,1:T(8,128)}, f32[4,1,64]{0,2,1:T(8,128)S(1)}, u32[]{:S(2)}) copy-start(f32[4,1,64]{0,2,1:T(8,128)S(1)} %copy.18) | copy-start | bytes 3076
  52.6 0.6 copy-start.7
  54.4 11.0 %all-to-all-start.1 = ((f32[4,16,4]{2,0,1:T(4,128)}), f32[4,16,4]{2,0,1:T(4,128)S(1)}, u32[]{:S(2)}, u32[]{:S(2)}) async-start(f32[4,16,4]{2,0,1:T(4,128)} %copy.14), calls=%async_computation.1 | async-start | bytes 65536 | tf_op jit(solution)/shard_map/all_to_all | solution.py:44
  57.9 228.8 %all-reduce.3.cloned.1.call-start = ((), (), s32[]{:S(2)}) async-start(), calls=%async_computation.2 | async-start | bytes 786432 | tf_op jit(solution)/shard_map/psum | solution.py:67
  65.5 1.1 copy-start.10
  67.4 1.0 copy-start.2
  67.4 1.0 copy-start.4
  68.4 1.1 copy-start.11
  69.5 1.1 copy-start.10
  71.4 1.0 copy-start.2
  71.4 1.0 copy-start.4
  72.4 1.1 copy-start.11
  73.5 1.1 copy-start.10
  75.4 1.0 copy-start.2
  75.4 1.0 copy-start.4
  76.4 1.1 copy-start.11
  77.5 1.1 copy-start.10
  79.4 1.0 copy-start.2
  79.4 1.0 copy-start.4
  80.4 1.1 copy-start.11
  83.8 202.9 %copy-start.8 = (f32[4]{0:T(128)S(1)}, f32[4]{0:T(128)}, u32[]{:S(2)}) copy-start(f32[4]{0:T(128)} %copy-done.7) | copy-start | bytes 52
  83.8 202.9 %copy-start.9 = (f32[4]{0:T(128)S(1)}, f32[4]{0:T(128)}, u32[]{:S(2)}) copy-start(f32[4]{0:T(128)} %get-tuple-element.60) | copy-start | bytes 52
  86.2 318.7 %all-reduce.5.cloned.1.call-start = ((), (), s32[]{:S(2)}) async-start(), calls=%async_computation.3 | async-start | bytes 786432 | tf_op jit(solution)/shard_map/psum | solution.py:67
Sparse Core Ops, SparseCore 0:
  86.3 200.3 all-reduce.2
  290.3 114.6 all-reduce.4
